TPU v7x, 32 devices: a whole 2x2x4 slice. The times are simulated.
32 devices in a mesh: dp: 8 (over z, x), shard: 4 (over y, core).
Axes of the slice: x: 2, y: 2, z: 4, core: 2. Of those that a mesh axis runs over, the one named last changes fastest.
Arguments:
- images: bfloat16 [8, 591, 768], P('dp'), may hold values from -6 to 6
- out_grad: bfloat16 [8, 591, 768], P('dp'), may hold values from -6 to 6
- slot_kind: int32 [8], P('dp'), may hold values from 0 to 1
- small_index: int32 [197, 197], replicated, may hold values from 0 to 731, as said below
- large_index: int32 [577, 577], replicated, may hold values from 0 to 2211, as said below
- qkv_weight: bfloat16 [768, 3, 768], P('dp', None, 'shard'), may hold values from -0.21875 to 0.21875
- out_weight: bfloat16 [768, 768], P('shard', 'dp'), may hold values from -1.75 to 1.75
- fc1_weight: bfloat16 [768, 3072], P('dp', 'shard'), may hold values from -0.21875 to 0.21875
- fc2_weight: bfloat16 [3072, 768], P('shard', 'dp'), may hold values from -0.109375 to 0.109375
- norm1_gain: bfloat16 [768], P('dp'), may hold values from 0.099609375 to 1.8984375
- norm1_shift: bfloat16 [768], P('dp'), may hold values from -1.796875 to 1.796875
- query_bias: bfloat16 [768], P('shard'), may hold values from -1.796875 to 1.796875
- value_bias: bfloat16 [768], P('shard'), may hold values from -1.796875 to 1.796875
- out_bias: bfloat16 [768], P('dp'), may hold values from -1.796875 to 1.796875
- gamma_attn: bfloat16 [768], P('dp'), may hold values from 0.099609375 to 1.8984375
- norm2_gain: bfloat16 [768], P('dp'), may hold values from 0.099609375 to 1.8984375
- norm2_shift: bfloat16 [768], P('dp'), may hold values from -1.796875 to 1.796875
- fc1_bias: bfloat16 [3072], P('shard'), may hold values from -1.796875 to 1.796875
- fc2_bias: bfloat16 [768], P('dp'), may hold values from -1.796875 to 1.796875
- gamma_mlp: bfloat16 [768], P('dp'), may hold values from 0.099609375 to 1.8984375
- small_table: bfloat16 [732, 12], P(None, 'shard'), may hold values from -4 to 4
- large_table: bfloat16 [2212, 12], P(None, 'shard'), may hold values from -4 to 4
Outputs:
- layer_out: bfloat16 [8, 591, 768], P('dp')
- input_grad: bfloat16 [8, 591, 768], P('dp')
- qkv_weight_grad: float32 [768, 3, 768], P('dp', None, 'shard')
- out_weight_grad: float32 [768, 768], P('shard', 'dp')
- fc1_weight_grad: float32 [768, 3072], P('dp', 'shard')
- fc2_weight_grad: float32 [3072, 768], P('shard', 'dp')
- norm1_gain_grad: float32 [768], P('dp')
- norm1_shift_grad: float32 [768], P('dp')
- query_bias_grad: float32 [768], P('shard')
- value_bias_grad: float32 [768], P('shard')
- out_bias_grad: float32 [768], P('dp')
- gamma_attn_grad: float32 [768], P('dp')
- norm2_gain_grad: float32 [768], P('dp')
- norm2_shift_grad: float32 [768], P('dp')
- fc1_bias_grad: float32 [3072], P('shard')
- fc2_bias_grad: float32 [768], P('dp')
- gamma_mlp_grad: float32 [768], P('dp')
- small_table_grad: float32 [732, 12], P(None, 'shard')
- large_table_grad: float32 [2212, 12], P(None, 'shard')
Inputs may be any that keep to these rules, and one draw needn't show every extreme that they name: `slot_kind`: 0: three images of 197 rows; 1: one image of 577 rows. `small_index`: every entry of the table is named by some pair. `large_index`: every entry of the table is named by some pair.
All inputs are finite; a program needn't handle non-finite values.
Results may differ from a plain program's by a relative error of at most 0.012.
The roundings to bfloat16 on the way count: a program that leaves them out, or rounds other values in their place, can miss the bound.
Values may be sent and summed in bfloat16 or wider, within the bound.
A program may use at most 384 MiB of HBM per device.

v0:
```python
import functools
import types

import jax
import jax.numpy as jnp
from jax import lax
from jax.experimental import pallas as pl
from jax.experimental.pallas import tpu as pltpu
from jax.sharding import PartitionSpec as P

HEAD_DIM = 64
SMALL_LEN = 197
LARGE_LEN = 577
SLOT_ROWS = 591
EPS = 1e-06
NEG = -1e30
LANES = 128
SPLIT = 80
VMEM_LIMIT = 56 << 20

MESH = pl.DeviceIdType.MESH

f32 = jnp.float32
bf16 = jnp.bfloat16


def up_to(value, unit):
    return -(-value // unit) * unit


def in_vmem(count):
    return [pl.BlockSpec(memory_space=pltpu.VMEM)] * count


def params(**more):
    return pltpu.CompilerParams(vmem_limit_bytes=VMEM_LIMIT, **more)


def dot(a, b, da, db):
    return lax.dot_general(a, b, (((da,), (db,)), ((), ())), preferred_element_type=f32)


def bias_block_of(heads, index_ref, table_ref, out_ref, here):
    columns, entries = index_ref.shape[1], table_ref.shape[1]
    for c in range(columns // LANES):
        there = pl.ds(c * LANES, LANES)
        index = index_ref[here, there]
        high = lax.shift_right_arithmetic(index, 7)
        low = lax.bitwise_and(index, LANES - 1)
        found = [jnp.full(index.shape, NEG, f32) for _ in range(heads)]
        for k in range(entries // LANES):
            match = high == k
            for h in range(heads):
                line = table_ref[h : h + 1, k * LANES : (k + 1) * LANES]
                values = jnp.take_along_axis(jnp.broadcast_to(line, index.shape), low, axis=1)
                found[h] = jnp.where(match, values, found[h])
        for h in range(heads):
            out_ref[h, here, there] = found[h].astype(bf16)


def table_block(heads, groups, index_ref, grad_ref, out_ref, here):
    columns = index_ref.shape[1]
    inverse = -(-(1 << 22) // SPLIT)
    index = index_ref[here, :]
    high = lax.shift_right_arithmetic(index * inverse, 22)
    low = (index - high * SPLIT).astype(jnp.int16)
    high = high.astype(jnp.int16)
    grads = [grad_ref[h, here, :] for h in range(heads)]
    places_low = lax.broadcasted_iota(jnp.int16, (SPLIT, columns), 0)
    places_high = lax.broadcasted_iota(jnp.int16, (groups, columns), 0)
    one, zero = jnp.ones((), bf16), jnp.zeros((), bf16)
    total = jnp.zeros((heads * groups, SPLIT), f32)
    for pair in range(0, 16, 2):
        lows, highs = [], []
        for i in (pair, pair + 1):
            lows.append(
                jnp.where(
                    places_low == jnp.broadcast_to(low[i : i + 1], (SPLIT, columns)), one, zero
                )
            )
            match = places_high == jnp.broadcast_to(high[i : i + 1], (groups, columns))
            highs.append(
                jnp.concatenate(
                    [
                        jnp.where(
                            match,
                            jnp.broadcast_to(grads[h][i : i + 1], (groups, columns)),
                            zero,
                        )
                        for h in range(heads)
                    ],
                    0,
                )
            )
        total = total + dot(jnp.concatenate(highs, 1), jnp.concatenate(lows, 1), 1, 1)
    out_ref[: heads * groups, :SPLIT] += total


def forward_body(heads, q_ref, k_ref, v_ref, bias_ref, out_ref):
    rows = q_ref.shape[0]
    for h in range(heads):
        part = slice(h * HEAD_DIM, (h + 1) * HEAD_DIM)
        scores = dot(q_ref[:, part], k_ref[:, part], 1, 1) * HEAD_DIM ** (-0.5)
        scores = scores + bias_ref[h, :, :rows].astype(f32)
        weights = jnp.exp(scores - jnp.max(scores, -1, keepdims=True))
        weights = weights / jnp.sum(weights, -1, keepdims=True)
        out_ref[:, part] = dot(weights.astype(bf16), v_ref[:, part], 1, 0).astype(bf16)


def backward_body(
    heads, q_ref, k_ref, v_ref, bias_ref, grad_ref, dq_ref, dk_ref, dv_ref, ds_ref
):
    rows = q_ref.shape[0]
    factor = HEAD_DIM ** (-0.5)
    for h in range(heads):
        part = slice(h * HEAD_DIM, (h + 1) * HEAD_DIM)
        scores = dot(q_ref[:, part], k_ref[:, part], 1, 1) * factor
        scores = scores + bias_ref[h, :, :rows].astype(f32)
        weights = jnp.exp(scores - jnp.max(scores, -1, keepdims=True))
        weights = weights / jnp.sum(weights, -1, keepdims=True)
        dv_ref[:, part] = dot(weights.astype(bf16), grad_ref[:, part], 0, 0).astype(bf16)
        grad = dot(grad_ref[:, part], v_ref[:, part], 1, 1)
        mean = jnp.sum(weights * grad, -1, keepdims=True)
        grad = (weights * (grad - mean)).astype(bf16)
        ds_ref[h, :, :rows] = grad
        dq_ref[:, part] = (dot(grad, k_ref[:, part], 1, 0) * factor).astype(bf16)
        dk_ref[:, part] = (dot(grad, q_ref[:, part], 0, 0) * factor).astype(bf16)


def attend_forward(queries, keys, values, bias):
    heads = bias.shape[0]
    return pl.pallas_call(
        functools.partial(forward_body, heads),
        out_shape=jax.ShapeDtypeStruct(queries.shape, bf16),
        in_specs=in_vmem(4),
        out_specs=in_vmem(1)[0],
        compiler_params=params(),
        cost_estimate=pl.CostEstimate(flops=10**9, bytes_accessed=10**7, transcendentals=10**6),
        name="attend_forward",
    )(queries, keys, values, bias)


def attend_backward(queries, keys, values, bias, grad):
    heads = bias.shape[0]
    rows = jax.ShapeDtypeStruct(queries.shape, bf16)
    return pl.pallas_call(
        functools.partial(backward_body, heads),
        out_shape=(rows, rows, rows, jax.ShapeDtypeStruct(bias.shape, bf16)),
        in_specs=in_vmem(5),
        out_specs=tuple(in_vmem(4)),
        compiler_params=params(),
        cost_estimate=pl.CostEstimate(flops=2 * 10**9, bytes_accessed=2 * 10**7, transcendentals=10**6),
        name="attend_backward",
    )(queries, keys, values, bias, grad)


def bias_body(heads, index_ref, table_ref, out_ref):
    def work(block):
        here = pl.ds(pl.multiple_of(block * ROW_STEP, ROW_STEP), ROW_STEP)
        bias_block_of(heads, index_ref, table_ref, out_ref, here)

    with_events(index_ref.shape[0] // ROW_STEP, [], work)


def gather_bias(pair_index, table):
    heads, entries = table.shape
    return pl.pallas_call(
        functools.partial(bias_body, heads),
        out_shape=jax.ShapeDtypeStruct((heads,) + pair_index.shape, bf16),
        in_specs=in_vmem(2),
        out_specs=in_vmem(1)[0],
        compiler_params=params(),
        cost_estimate=pl.CostEstimate(flops=10**9, bytes_accessed=4 * 10**7, transcendentals=0),
        name="bias",
    )(pair_index, table)


def table_body(heads, groups, index_ref, grad_ref, out_ref):
    out_ref[...] = jnp.zeros_like(out_ref)

    def work(block):
        here = pl.ds(pl.multiple_of(block * ROW_STEP, ROW_STEP), ROW_STEP)
        table_block(heads, groups, index_ref, grad_ref, out_ref, here)

    with_events(index_ref.shape[0] // ROW_STEP, [], work)


def table_sums(pair_index, grad_scores, entries):
    heads = grad_scores.shape[0]
    groups = up_to(-(-entries // SPLIT), 16)
    sums = pl.pallas_call(
        functools.partial(table_body, heads, groups),
        out_shape=jax.ShapeDtypeStruct((heads * groups, SPLIT), f32),
        in_specs=in_vmem(2),
        out_specs=in_vmem(1)[0],
        compiler_params=params(),
        cost_estimate=pl.CostEstimate(flops=2 * 10**9, bytes_accessed=6 * 10**7, transcendentals=0),
        name="table_sums",
    )(pair_index, grad_scores)
    return sums.reshape(heads, groups * SPLIT)


def cuts_of(total, pieces, unit=16):
    count, extra = divmod(total // unit, pieces)
    cuts, at = [], 0
    for i in range(pieces):
        size = (count + (i < extra)) * unit
        if size:
            cuts.append((at, size))
        at += size
    return cuts


def remote(src, dst, send_sem, recv_sem, axis, peer):
    return pltpu.make_async_remote_copy(
        src_ref=src,
        dst_ref=dst,
        send_sem=send_sem,
        recv_sem=recv_sem,
        device_id={axis: peer},
        device_id_type=MESH,
    )


def greet(barrier, axis, peer):
    pl.semaphore_signal(barrier, inc=1, device_id={axis: peer}, device_id_type=MESH)


class ShardSum:
    def __init__(self, chunks, part_ref, out_ref, near, sent, far, send_sem, recv_sem):
        me = lax.axis_index("shard")
        outer, self.inner = me // 2, lax.rem(me, 2)
        self.near_peer = outer * 2 + (1 - self.inner)
        self.far_peer = (1 - outer) * 2 + self.inner
        self.chunks, self.part, self.out = chunks, part_ref, out_ref
        self.near, self.sent, self.far = near, sent, far
        self.sems = (send_sem, recv_sem)
        self.half = near.shape[0]

    def greet(self, barrier):
        greet(barrier, "shard", self.near_peer)
        greet(barrier, "shard", self.far_peer)
        return 2

    def rows(self, which, at, size):
        return pl.ds(pl.multiple_of(which * self.half + at, 16), size)

    def copy(self, stage, j, src, dst, peer):
        send_sem, recv_sem = self.sems
        return remote(src, dst, send_sem.at[stage, j], recv_sem.at[stage, j], "shard", peer)

    def first(self, j):
        at, size = self.chunks[j]
        return self.copy(
            0, j, self.part.at[self.rows(1 - self.inner, at, size)], self.near.at[pl.ds(at, size)], self.near_peer
        )

    def second(self, j):
        here = pl.ds(*self.chunks[j])
        return self.copy(1, j, self.sent.at[here], self.far.at[here], self.far_peer)

    def third(self, j):
        mine = self.out.at[self.rows(self.inner, *self.chunks[j])]
        return self.copy(2, j, mine, mine, self.near_peer)

    def start(self):
        for j in range(len(self.chunks)):
            self.first(j).start()

    def cross_one(self, j):
        at, size = self.chunks[j]
        self.first(j).wait_recv()
        here = pl.ds(at, size)
        mine = self.rows(self.inner, at, size)
        self.sent[here] = (self.part[mine] + self.near[here]).astype(bf16)
        self.second(j).start()

    def cross(self):
        for j in range(len(self.chunks)):
            self.cross_one(j)

    def close_one(self, j):
        at, size = self.chunks[j]
        self.second(j).wait_recv()
        here = pl.ds(at, size)
        mine = self.rows(self.inner, at, size)
        self.out[mine] = self.sent[here].astype(f32) + self.far[here].astype(f32)
        self.third(j).start()

    def close(self):
        for j in range(len(self.chunks)):
            self.close_one(j)

    def arrive(self):
        for j in range(len(self.chunks)):
            self.third(j).wait_recv()

    def drain(self):
        for j in range(len(self.chunks)):
            self.first(j).wait_send()
            self.second(j).wait_send()
            self.third(j).wait_send()


class Grid:
    def __init__(self, peers):
        self.length = peers // 2
        self.me = lax.axis_index("dp")
        self.at, self.side = self.me // 2, lax.rem(self.me, 2)
        self.up, self.down = self.me + 2, self.me - 2
        self.across = self.at * 2 + 1 - self.side
        self.has_up, self.has_down = self.at < self.length - 1, self.at > 0

    def greet(self, barrier):
        greet(barrier, "dp", self.across)

        @pl.when(self.has_up)
        def _():
            greet(barrier, "dp", self.up)

        @pl.when(self.has_down)
        def _():
            greet(barrier, "dp", self.down)

        return 1 + self.has_up.astype(jnp.int32) + self.has_down.astype(jnp.int32)

    def clip(self, place):
        return jnp.clip(place, 0, self.length - 1)


class Flood:
    def __init__(self, grid, own, out, up_send, up_recv, down_send, down_recv, side_send, side_recv):
        self.grid, self.own, self.out = grid, own, out
        self.up_sems, self.down_sems = (up_send, up_recv), (down_send, down_recv)
        self.side_sems = (side_send, side_recv)

    def at(self, device):
        depth = self.own.shape[0]
        return self.out.at[pl.ds(pl.multiple_of(device * depth, 8), depth)]

    def block(self, place):
        return self.at(self.grid.clip(place) * 2 + self.grid.side)

    def up(self, s):
        grid, (send, recv) = self.grid, self.up_sems
        block = self.block(grid.at - s)
        return remote(self.own if s == 0 else block, block, send.at[s], recv.at[s], "dp", grid.up)

    def down(self, s):
        grid, (send, recv) = self.grid, self.down_sems
        block = self.block(grid.at + s)
        return remote(self.own if s == 0 else block, block, send.at[s], recv.at[s], "dp", grid.down)

    def across(self, place, own=False):
        grid, (send, recv) = self.grid, self.side_sems
        place = grid.clip(place)
        block = self.block(place)
        return remote(
            self.own if own else block, block, send.at[place], recv.at[place], "dp", grid.across
        )

    def step(self, s):
        grid = self.grid
        if s == 0:

            @pl.when(grid.has_up)
            def _():
                self.up(0).start()

            @pl.when(grid.has_down)
            def _():
                self.down(0).start()

            self.across(grid.at, own=True).start()
            return

        @pl.when(grid.at - s >= 0)
        def _():
            block = self.block(grid.at - s)
            send, recv = self.up_sems
            remote(block, block, send.at[s - 1], recv.at[s - 1], "dp", grid.down).wait_recv()

            @pl.when(grid.has_up)
            def _():
                self.up(s).start()

            self.across(grid.at - s).start()

        @pl.when(grid.at + s < grid.length)
        def _():
            block = self.block(grid.at + s)
            send, recv = self.down_sems
            remote(block, block, send.at[s - 1], recv.at[s - 1], "dp", grid.up).wait_recv()

            @pl.when(grid.has_down)
            def _():
                self.down(s).start()

            self.across(grid.at + s).start()

    def arrive(self):
        grid, (send, recv) = self.grid, self.side_sems
        for place in range(grid.length):
            block = self.at(place * 2 + 1 - grid.side)
            remote(block, block, send.at[place], recv.at[place], "dp", grid.across).wait_recv()

    def drain(self):
        grid = self.grid
        for place in range(grid.length):
            self.across(place).wait_send()
        for s in range(grid.length - 1):

            @pl.when(jnp.logical_and(grid.at - s >= 0, grid.has_up))
            def _():
                self.up(s).wait_send()

            @pl.when(jnp.logical_and(grid.at + s < grid.length, grid.has_down))
            def _():
                self.down(s).wait_send()


SIDE, UP, DOWN = range(3)


class ReduceScatter:
    def __init__(self, grid, grads, out, side, up, down, sems):
        self.grid, self.grads, self.out = grid, grads, out
        self.buffers = (side, up, down)
        self.sems = (sems[:2], sems[2:4], sems[4:6])

    def at(self, device):
        depth = self.out.shape[0]
        return pl.ds(pl.multiple_of(device * depth, 16), depth)

    def prepare(self):
        grid = self.grid

        @pl.when(jnp.logical_not(grid.has_down))
        def _():
            self.buffers[UP][...] = jnp.zeros_like(self.buffers[UP])

        @pl.when(jnp.logical_not(grid.has_up))
        def _():
            self.buffers[DOWN][...] = jnp.zeros_like(self.buffers[DOWN])

    def copy(self, way, place, peer, src=None):
        send, recv = self.sems[way]
        place = self.grid.clip(place)
        dst = self.buffers[way].at[place]
        return remote(dst if src is None else src, dst, send.at[place], recv.at[place], "dp", peer)

    def cross(self, place):
        grid = self.grid
        src = self.grads.at[self.at(grid.clip(place) * 2 + 1 - grid.side)]
        return self.copy(SIDE, place, grid.across, src)

    def start(self, s):
        grid = self.grid

        @pl.when(grid.at + s < grid.length)
        def _():
            self.cross(grid.at + s).start()

        if s:

            @pl.when(grid.at - s >= 0)
            def _():
                self.cross(grid.at - s).start()

    def step(self, s):
        grid = self.grid
        side, up, down = self.buffers
        if s == 0:
            place = grid.at
            self.copy(SIDE, place, grid.across).wait_recv()

            @pl.when(grid.has_down)
            def _():
                self.copy(UP, place, grid.down).wait_recv()

            @pl.when(grid.has_up)
            def _():
                self.copy(DOWN, place, grid.up).wait_recv()

            total = self.grads[self.at(grid.me)].astype(f32) + side[place].astype(f32)
            self.out[...] = total + (up[place].astype(f32) + down[place].astype(f32))
            return

        @pl.when(grid.at + s < grid.length)
        def _():
            place = grid.clip(grid.at + s)
            self.copy(SIDE, place, grid.across).wait_recv()

            @pl.when(grid.has_down)
            def _():
                self.copy(UP, place, grid.down).wait_recv()

            total = self.grads[self.at(place * 2 + grid.side)].astype(f32) + side[place].astype(f32)
            side[place] = (total + up[place].astype(f32)).astype(bf16)
            self.copy(UP, place, grid.up, side.at[place]).start()

        @pl.when(grid.at - s >= 0)
        def _():
            place = grid.clip(grid.at - s)
            self.copy(SIDE, place, grid.across).wait_recv()

            @pl.when(grid.has_up)
            def _():
                self.copy(DOWN, place, grid.up).wait_recv()

            total = self.grads[self.at(place * 2 + grid.side)].astype(f32) + side[place].astype(f32)
            side[place] = (total + down[place].astype(f32)).astype(bf16)
            self.copy(DOWN, place, grid.down, side.at[place]).start()

    def drain(self):
        grid = self.grid
        for place in range(grid.length):
            self.cross(place).wait_send()
        for s in range(1, grid.length):

            @pl.when(grid.at + s < grid.length)
            def _():
                self.copy(UP, grid.at + s, grid.up).wait_send()

            @pl.when(grid.at - s >= 0)
            def _():
                self.copy(DOWN, grid.at - s, grid.down).wait_send()


ROW_STEP = 16
CHUNKS = 5
VECTORS = 8
EARLY_LINES = 16
LAG = 0
BIAS_PLACES = [5, 11, 17, 11, 19, 25, 32, 20, 28, 36, 99]
TABLE_PLACES = [1, 3, 10, 15, 20, 24, 30, 36, 99]
CLOSE_PLACE = 17
NORM_PLACE = 22


def with_events(blocks, events, work):
    def step(block, carry):
        for at, event in events:
            pl.when(block == at)(event)

        @pl.when(block < blocks)
        def _():
            work(block)

        return carry

    lax.fori_loop(0, max([blocks] + [at + 1 for at, _ in events]), step, 0)


class Spread:
    def __init__(self, peers, out, send_sem, recv_sem):
        self.peers, self.out, self.sems = peers, out, (send_sem, recv_sem)
        self.me = lax.axis_index("dp")

    def peer(self, i):
        return lax.rem(self.me + i, self.peers)

    def copy(self, src, slot, peer):
        send_sem, recv_sem = self.sems
        return remote(
            src, self.out.at[slot], send_sem.at[peer], recv_sem.at[slot], "dp", peer
        )

    def start(self, src_for):
        for i in range(1, self.peers):
            self.copy(src_for(self.peer(i)), self.me, self.peer(i)).start()

    def arrive(self):
        for i in range(1, self.peers):
            peer = self.peer(i)
            self.copy(self.out.at[peer], peer, peer).wait_recv()

    def drain(self):
        for i in range(1, self.peers):
            peer = self.peer(i)
            self.copy(self.out.at[peer], peer, peer).wait_send()


def layer_body(plan, *refs):
    tree, heads, groups, slot_rows, peers = plan
    named = {}
    for part in jax.tree.unflatten(tree, refs):
        named.update(part)
    r = types.SimpleNamespace(**named)
    rows, columns = r.index.shape
    model = r.inputs.shape[1]
    depth = model // peers
    inner = heads * HEAD_DIM
    half = rows // 2
    chunks = cuts_of(half, CHUNKS)
    count = len(chunks)
    factor = HEAD_DIM ** (-0.5)
    height = heads * groups

    grid = Grid(peers)
    sums = [
        ShardSum(chunks, *buffers)
        for buffers in zip(r.part, r.total, r.near, r.sent, r.far, r.sum_send, r.sum_recv)
    ]
    lines = Flood(grid, r.own_lines, r.all_lines, *r.flood_sems[3])
    floods = [
        Flood(grid, own, out, *sems) for own, out, sems in zip((r.own_first, r.fc1_weight, r.fc2_weight), r.whole, r.flood_sems)
    ]
    scatters = [
        ReduceScatter(grid, *buffers)
        for buffers in zip(r.grad, r.summed, r.side, r.up, r.down, r.scatter_sems)
    ]
    spreads = [
        Spread(peers, out, *sems)
        for out, sems in zip((r.all_early, r.all_late, r.all_table), r.spread_sems)
    ]

    loads = [
        pltpu.make_async_copy(src, dst, r.load_sem.at[j])
        for j, (src, dst) in enumerate(
            ((r.large_index, r.wide_from), (r.inputs, r.inputs_here), (r.out_grad, r.grad_here))
        )
    ]
    for load in loads:
        load.start()
    for i, member in enumerate(r.small_vectors):
        r.own_lines[i : i + 1, :depth] = member[...].astype(f32).reshape(1, depth)
    for j in range(3):
        r.own_first[:, j * inner : (j + 1) * inner] = r.qkv_weight[j]
    r.own_first[:, 3 * inner :] = r.out_weight[...].T
    barrier = pltpu.get_barrier_semaphore()
    met = sums[0].greet(barrier)
    for i in range(1, peers):
        greet(barrier, "dp", lax.rem(grid.me + i, peers))
    pl.semaphore_wait(barrier, met + peers - 1)
    lines.step(0)
    floods[0].step(0)
    copies = [
        pltpu.make_async_copy(flood.own, flood.at(grid.me), r.local_sem.at[j])
        for j, flood in enumerate(floods + [lines])
    ]
    for copy in copies:
        copy.start()
    for scatter in scatters:
        scatter.prepare()

    kind = r.slot_kind[0]
    r.slot[0:1] = jnp.full((1, LANES), kind.astype(f32))
    r.slot[1:2] = jnp.full((1, LANES), (slot_rows - kind * (slot_rows - LARGE_LEN)).astype(f32))
    is_large = jnp.broadcast_to(r.slot[0:1, :], (8, LANES)) > 0.5
    small_side, large_side = r.small_index.shape[0], r.large_index.shape[0]
    r.index[...] = jnp.full((rows, columns), -1, jnp.int32)
    for image in range(slot_rows // small_side):
        at = image * small_side
        r.index[at : at + small_side, at : at + small_side] = r.small_index[...]
    r.wide_index[...] = jnp.full((rows, columns), -1, jnp.int32)
    for load in loads:
        load.wait()
    r.wide_index[:large_side, :large_side] = r.wide_from[...]
    r.table[...] = jnp.zeros_like(r.table)
    entries_small, entries_large = r.small_table.shape[1], r.large_table.shape[1]
    r.table[:heads, :entries_small] = r.small_table[...].astype(f32)
    r.wide_table[...] = jnp.zeros_like(r.wide_table)
    r.wide_table[:heads, :entries_large] = r.large_table[...].astype(f32)
    tall = jnp.broadcast_to(is_large[:, 0:1], r.table.shape)
    r.table[...] = jnp.where(tall, r.wide_table[...], r.table[...])
    large_block = jnp.broadcast_to(r.slot[0:1, 0:1], (ROW_STEP, columns)) > 0.5

    body_rows = slot_rows // 32 * 32
    tail = slot_rows - body_rows
    r.kept[:body_rows] = r.inputs_here[:body_rows]
    r.kept[body_rows:] = jnp.concatenate(
        (
            r.inputs_here[body_rows:slot_rows].astype(f32),
            jnp.zeros((rows - slot_rows, model), f32),
        ),
        0,
    ).astype(bf16)
    blocks = up_to(slot_rows, ROW_STEP) // ROW_STEP

    def bias_block(block):
        here = pl.ds(pl.multiple_of(block * ROW_STEP, ROW_STEP), ROW_STEP)
        r.index[here] = jnp.where(large_block, r.wide_index[here], r.index[here])
        bias_block_of(heads, r.index, r.table, r.bias, here)

    r.index[blocks * ROW_STEP :] = jnp.full((rows - blocks * ROW_STEP, columns), -1, jnp.int32)
    r.bias[:, blocks * ROW_STEP :] = jnp.full(
        (heads, rows - blocks * ROW_STEP, columns), NEG, bf16
    )
    length = grid.length

    def flood_event(j, s):
        return lambda: floods[j].step(s)

    order = [(0, s) for s in range(1, length)] + [(j, s) for j in (1, 2) for s in range(length)]
    places = BIAS_PLACES if length == 4 else [k * 3 for k in range(len(order))]
    events = [(at, flood_event(*item)) for at, item in zip(places, order)]
    events += [(3 * s, functools.partial(lines.step, s)) for s in range(1, length)]
    late_floods = [event for at, event in events if at >= blocks]
    with_events(blocks, [(at, event) for at, event in events if at < blocks], bias_block)
    for copy in copies:
        copy.wait()
    lines.arrive()
    floods[0].arrive()
    for d in range(peers):
        r.vectors[:, d * depth : (d + 1) * depth] = r.all_lines[
            d * VECTORS : (d + 1) * VECTORS, :depth
        ]

    def vector(i):
        return r.vectors[i : i + 1, :]

    def moments(value):
        mean = jnp.mean(value, -1, keepdims=True)
        center = value - mean
        inverse = lax.rsqrt(jnp.mean(center * center, -1, keepdims=True) + EPS)
        return center * inverse, mean, inverse

    def both(ref, c):
        at, size = chunks[c]
        return jnp.concatenate((ref[at : at + size], ref[half + at : half + at + size]), 0)

    def put(ref, c, value):
        at, size = chunks[c]
        ref[at : at + size] = value[:size]
        ref[half + at : half + at + size] = value[size:]

    def add(i, value):
        r.running[i] += value.reshape(value.shape[0] // 8, 8, value.shape[1]).sum(0)

    r.running[...] = jnp.zeros_like(r.running)
    r.qkv_shift[...] = jnp.zeros_like(r.qkv_shift)
    r.qkv_shift[:, :inner] = r.query_bias[...].astype(f32).reshape(1, inner)
    r.qkv_shift[:, 2 * inner :] = r.value_bias[...].astype(f32).reshape(1, inner)
    r.hidden_shift[...] = r.fc1_bias[...].astype(f32).reshape(r.hidden_shift.shape)
    for c in range(count):
        normal, mean, inverse = moments(both(r.kept, c).astype(f32))
        put(r.mean[0], c, mean)
        put(r.inverse[0], c, inverse)
        normed = (normal * vector(0) + vector(1)).astype(bf16)
        put(r.normed[0], c, normed)
        projected = dot(normed, r.whole[0][:, : 3 * inner], 1, 0) + r.qkv_shift[...]
        put(r.qkv, c, projected.astype(bf16))

    def weights_of(h):
        part = slice(h * HEAD_DIM, (h + 1) * HEAD_DIM)
        keys = slice(inner + h * HEAD_DIM, inner + (h + 1) * HEAD_DIM)
        scores = dot(r.qkv[:, part], r.qkv[:, keys], 1, 1) * factor
        scores = scores + r.bias[h, :, :rows].astype(f32)
        weights = jnp.exp(scores - jnp.max(scores, -1, keepdims=True))
        return weights * (1.0 / jnp.sum(weights, -1, keepdims=True))

    for h in range(heads):
        for event in late_floods[h * len(late_floods) // heads : (h + 1) * len(late_floods) // heads]:
            event()
        part = slice(h * HEAD_DIM, (h + 1) * HEAD_DIM)
        values = slice(2 * inner + h * HEAD_DIM, 2 * inner + (h + 1) * HEAD_DIM)
        r.attended[:, part] = dot(weights_of(h).astype(bf16), r.qkv[:, values], 1, 0).astype(bf16)

    def out_turned():
        return r.whole[0][:, 3 * inner :]

    def live_rows(c):
        at, size = chunks[c]
        first = lax.broadcasted_iota(jnp.int32, (size, 1), 0) + at
        places = jnp.concatenate((first, first + half), 0).astype(f32)
        return jnp.where(places < r.slot[1:2, 0:1], 1.0, 0.0)

    def padded(ref, c):
        at, size = chunks[c]
        last = min(half + at + size, slot_rows)
        low = ref[half + at : last]
        missing = half + at + size - last
        if missing:
            low = jnp.concatenate(
                (low.astype(f32), jnp.zeros((missing, low.shape[1]), f32)), 0
            )
        return jnp.concatenate((ref[at : at + size].astype(f32), low.astype(f32)), 0)

    def keep(ref, c, value):
        at, size = chunks[c]
        last = min(half + at + size, slot_rows)
        ref[at : at + size] = value[:size]
        ref[half + at : last] = value[size : size + last - half - at]

    def project(c):
        put(r.part[0], c, dot(both(r.attended, c), out_turned(), 1, 1))
        sums[0].first(c).start()

    def forward(c):
        if c == 0:
            floods[1].arrive()
        sums[0].third(c).wait_recv()
        middle = both(r.kept, c).astype(f32) + vector(3) * (both(r.total[0], c) + vector(2))
        put(r.middle, c, middle)
        normal, mean, inverse = moments(middle)
        put(r.mean[1], c, mean)
        put(r.inverse[1], c, inverse)
        normed = (normal * vector(4) + vector(5)).astype(bf16)
        put(r.normed[1], c, normed)
        hidden = dot(normed, r.whole[1][...], 1, 0) + r.hidden_shift[...]
        cumulative = 0.5 * (1.0 + lax.erf(hidden * 0.7071067811865476))
        put(
            r.slope,
            c,
            cumulative + hidden * jnp.exp(-0.5 * hidden * hidden) * 0.3989422804014327,
        )
        active = (hidden * cumulative).astype(bf16)
        put(r.active, c, active)
        if c == 0:
            floods[2].arrive()
        put(r.part[1], c, dot(active, r.whole[2][...], 1, 1))
        sums[1].first(c).start()

    def turn(c):
        sums[1].third(c).wait_recv()
        result = both(r.total[1], c) + vector(6)
        live = live_rows(c)
        keep(r.out_here, c, (live * (both(r.middle, c) + vector(7) * result)).astype(bf16))
        grad = padded(r.grad_here, c) * live
        add(6, grad * result)
        grad_result = (grad * vector(7)).astype(bf16)
        put(r.grad_result, c, grad_result)
        add(5, grad_result.astype(f32))
        grad_hidden = (dot(grad_result, r.whole[2][...], 1, 0) * both(r.slope, c)).astype(bf16)
        put(r.grad_hidden, c, grad_hidden)
        add(0, grad_hidden.astype(f32))
        put(r.part[2], c, dot(grad_hidden, r.whole[1][...], 1, 1))
        sums[2].first(c).start()

    def back_norm(grad, normal, inverse, gain):
        scaled = grad * gain
        along = jnp.mean(scaled * normal, -1, keepdims=True)
        return inverse * (scaled - jnp.mean(scaled, -1, keepdims=True) - normal * along)

    def backward(c):
        sums[2].third(c).wait_recv()
        grad = both(r.total[2], c)
        inverse = both(r.inverse[1], c)
        normal = (both(r.middle, c) - both(r.mean[1], c)) * inverse
        add(3, grad * normal)
        add(4, grad)
        grad_middle = padded(r.grad_here, c) * live_rows(c)
        grad_middle = grad_middle + back_norm(grad, normal, inverse, vector(4))
        put(r.middle, c, grad_middle)
        add(2, grad_middle * (both(r.total[0], c) + vector(2)))
        grad_branch = (grad_middle * vector(3)).astype(bf16)
        put(r.grad_branch, c, grad_branch)
        add(1, grad_branch.astype(f32))
        put(r.grad_attended, c, dot(grad_branch, out_turned(), 1, 0).astype(bf16))

    def close(work):
        return lambda c: work.close_one(c)

    def cross(work):
        return lambda c: work.cross_one(c)

    stages = [project, cross(sums[0]), close(sums[0]), forward, cross(sums[1]), close(sums[1])]
    stages += [turn, cross(sums[2]), close(sums[2]), backward]

    def weight_grad(j, left, right, at=0):
        value = dot(left[...], right[...], 0, 0).astype(bf16)
        r.grad[j][:, at : at + value.shape[1]] = value

    def send_grads(j):
        for s in range(length - 1, -1, -1):
            scatters[j].start(s)

    slots = [0, 1, 2] + [k + LAG for k in range(3, 6)] + [k + 2 * LAG for k in range(6, 10)]
    for t in range(count + slots[-1]):
        for k in range(len(stages) - 1, -1, -1):
            if 0 <= t - slots[k] < count:
                stages[k](t - slots[k])
        if t == count + slots[6]:
            weight_grad(2, r.grad_result, r.active)
            send_grads(2)
        if t == count + slots[7]:
            weight_grad(1, r.normed[1], r.grad_hidden)
            send_grads(1)

    store = pltpu.make_async_copy(r.out_here, r.layer_out, r.load_sem.at[0])
    store.start()
    weight_grad(0, r.grad_branch, r.attended, 3 * inner)
    steps = list(range(length - 1, -1, -1))
    for h in range(heads):
        part = slice(h * HEAD_DIM, (h + 1) * HEAD_DIM)
        keys = slice(inner + h * HEAD_DIM, inner + (h + 1) * HEAD_DIM)
        values = slice(2 * inner + h * HEAD_DIM, 2 * inner + (h + 1) * HEAD_DIM)
        weights = weights_of(h)
        grad_part = r.grad_attended[:, part]
        r.grad_qkv[:, values] = dot(weights.astype(bf16), grad_part, 0, 0).astype(bf16)
        grad = dot(grad_part, r.qkv[:, values], 1, 1)
        mean = jnp.sum(weights * grad, -1, keepdims=True)
        grad = (weights * (grad - mean)).astype(bf16)
        r.bias[h, :, :rows] = grad
        r.grad_qkv[:, part] = (dot(grad, r.qkv[:, keys], 1, 0) * factor).astype(bf16)
        r.grad_qkv[:, keys] = (dot(grad, r.qkv[:, part], 0, 0) * factor).astype(bf16)
        if h + 1 < length:
            scatters[2].step(steps[h])

    sums[0].drain()
    last = sums[0]
    for c in range(count):
        put(r.part[0], c, dot(both(r.grad_qkv, c), r.whole[0][:, : 3 * inner], 1, 1))
        last.first(c).start()
    weight_grad(0, r.normed[0], r.grad_qkv)
    send_grads(0)

    wide = model // LANES
    at = 1
    r.own_early[...] = jnp.zeros_like(r.own_early)
    r.own_early[0:1] = r.slot[0:1, :]

    def line_to(at, line):
        for c in range(-(-line.shape[1] // LANES)):
            piece = line[:, c * LANES : (c + 1) * LANES]
            r.own_early[at + c : at + c + 1, : piece.shape[1]] = piece

    for line in (
        jnp.sum(r.running[0], 0, keepdims=True),
        jnp.sum(r.grad_qkv[:, :inner].astype(f32), 0, keepdims=True),
        jnp.sum(r.grad_qkv[:, 2 * inner :].astype(f32), 0, keepdims=True),
    ):
        line_to(at, line)
        at += up_to(line.shape[1], LANES) // LANES
    spreads[0].start(lambda peer: r.own_early)

    def to_owners(i, value):
        line = jnp.sum(value, 0, keepdims=True)
        for d in range(peers):
            r.own_late[d, i : i + 1, :depth] = line[:, d * depth : (d + 1) * depth]

    r.own_late[...] = jnp.zeros_like(r.own_late)
    for i in range(1, 7):
        to_owners(i - 1, r.running[i])
    r.table_sums[...] = jnp.zeros_like(r.table_sums)

    def norm_step(here, out_rows):
        grad = r.total[0][here]
        normal = (r.kept[here].astype(f32) - r.mean[0][here]) * r.inverse[0][here]
        back = back_norm(grad, normal, r.inverse[0][here], vector(0))
        value = (r.middle[here] + back).astype(bf16)
        if out_rows is None:
            r.input_grad[here] = value
        else:
            r.input_grad[out_rows] = value[:tail]
        product = (grad * normal).reshape(4, 8, model).sum(0)
        return product, grad.reshape(4, 8, model).sum(0)

    def norm_rows():
        last.arrive()

        def step(i, totals):
            gain, shift = norm_step(pl.ds(pl.multiple_of(i * 32, 32), 32), None)
            return totals[0] + gain, totals[1] + shift

        zero = jnp.zeros((8, model), f32)
        gain, shift = lax.fori_loop(0, body_rows // 32, step, (zero, zero))
        if tail:
            more = norm_step(slice(body_rows, rows), slice(body_rows, slot_rows))
            gain, shift = gain + more[0], shift + more[1]
        to_owners(6, gain)
        to_owners(7, shift)

    def scatter_event(j, s):
        return lambda: scatters[j].step(s)

    order = [(2, s) for s in steps[min(heads, length - 1) :]]
    order += [(j, s) for j in (1, 0) for s in steps]
    places = TABLE_PLACES if length == 4 else [4 * k for k in range(len(order))]
    events = [(at, scatter_event(*item)) for at, item in zip(places, order)]
    events += [(0, last.cross), (CLOSE_PLACE, last.close), (NORM_PLACE, norm_rows)]
    with_events(
        blocks,
        [(at, event) for at, event in events if at < blocks],
        lambda block: table_block(
            heads,
            groups,
            r.index,
            r.bias,
            r.table_sums,
            pl.ds(pl.multiple_of(block * ROW_STEP, ROW_STEP), ROW_STEP),
        ),
    )
    r.own_table[...] = r.table_sums[...].astype(bf16)
    spreads[2].start(lambda peer: r.own_table)
    spreads[1].start(lambda peer: r.own_late.at[peer])
    for at, event in events:
        if at >= blocks:
            event()
    r.all_early[grid.me] = r.own_early[...]
    r.all_late[grid.me] = r.own_late[grid.me]
    r.all_table[grid.me] = r.own_table[...]
    for spread in spreads:
        spread.arrive()
    early = jnp.zeros(r.early_sums.shape, f32)
    late = jnp.zeros(r.late_sums.shape, f32)
    small = jnp.zeros((height, LANES), f32)
    large = jnp.zeros((height, LANES), f32)
    for d in range(peers):
        kind = r.all_early[d, 0:1] > 0.5
        table = r.all_table[d].astype(f32)
        small += jnp.where(kind, 0.0, table)
        large += jnp.where(kind, table, 0.0)
        early += r.all_early[d]
        late += r.all_late[d]
    r.early_sums[...] = early
    r.late_sums[...] = late
    for out, value in ((r.small_sums, small), (r.large_sums, large)):
        entries = out.shape[1]
        for k in range(-(-entries // SPLIT)):
            first, size = k * SPLIT, min(SPLIT, entries - k * SPLIT)
            for h in range(heads):
                at = h * groups + k
                out[h : h + 1, first : first + size] = value[at : at + 1, :size]
    store.wait()
    for work in sums + floods + [lines] + scatters + spreads:
        work.drain()


def layer(arguments, peers, slot_rows):
    model = arguments["inputs"].shape[1]
    rows = up_to(slot_rows, 32)
    columns = up_to(rows, LANES)
    depth = model // peers
    hidden = arguments["fc1_bias"].shape[0]
    inner = arguments["query_bias"].shape[0]
    widths = [4 * inner, hidden, hidden]
    heads = inner // HEAD_DIM
    tables = [arguments["small_table"].shape, arguments["large_table"].shape]
    entries = up_to(max(shape[1] for shape in tables), LANES)
    groups = up_to(-(-entries // SPLIT), 16)
    height = heads * groups
    count = len(cuts_of(rows // 2, CHUNKS))
    length = peers // 2
    array = jax.ShapeDtypeStruct

    def sems(*shape):
        return pltpu.SemaphoreType.DMA(shape)

    def each(kind, shape, times):
        return [pltpu.VMEM(shape, kind) for _ in range(times)]

    outs = dict(
        layer_out=array((slot_rows, model), bf16),
        input_grad=array((slot_rows, model), bf16),
        small_sums=array(tables[0], f32),
        large_sums=array(tables[1], f32),
        early_sums=array((EARLY_LINES, LANES), f32),
        late_sums=array((VECTORS, LANES), f32),
        summed=[array((depth, w), f32) for w in widths],
    )
    blocks = [pltpu.VMEM((length, depth, w), bf16) for w in widths]
    scratch = dict(
        whole=[pltpu.VMEM((model, w), bf16) for w in widths],
        all_lines=pltpu.VMEM((peers * VECTORS, LANES), f32),
        grad=[pltpu.VMEM((model, w), bf16) for w in widths],
        side=blocks,
        up=blocks,
        down=blocks,
        scatter_sems=[[sems(length)] * 6] * 3,
        flood_sems=[[sems(length)] * 6] * 4,
        spread_sems=[[sems(peers)] * 2] * 3,
        part=each(f32, (rows, model), 3),
        total=each(f32, (rows, model), 3),
        near=each(f32, (rows // 2, model), 3),
        sent=each(bf16, (rows // 2, model), 3),
        far=each(bf16, (rows // 2, model), 3),
        sum_send=[sems(3, count)] * 3,
        sum_recv=[sems(3, count)] * 3,
        local_sem=sems(4),
        load_sem=sems(3),
        wide_from=pltpu.VMEM(arguments["large_index"].shape, jnp.int32),
        inputs_here=pltpu.VMEM((slot_rows, model), bf16),
        grad_here=pltpu.VMEM((slot_rows, model), bf16),
        out_here=pltpu.VMEM((slot_rows, model), bf16),
        own_first=pltpu.VMEM((depth, 4 * inner), bf16),
        own_lines=pltpu.VMEM((VECTORS, LANES), f32),
        slot=pltpu.VMEM((2, LANES), f32),
        hidden_shift=pltpu.VMEM((1, hidden), f32),
        index=pltpu.VMEM((rows, columns), jnp.int32),
        wide_index=pltpu.VMEM((rows, columns), jnp.int32),
        table=pltpu.VMEM((8, entries), f32),
        wide_table=pltpu.VMEM((8, entries), f32),
        bias=pltpu.VMEM((heads, rows, columns), bf16),
        vectors=pltpu.VMEM((VECTORS, model), f32),
        qkv_shift=pltpu.VMEM((1, 3 * inner), f32),
        running=pltpu.VMEM((7, 8, max(model, hidden)), f32),
        mean=each(f32, (rows, 1), 2),
        inverse=each(f32, (rows, 1), 2),
        normed=each(bf16, (rows, model), 2),
        kept=pltpu.VMEM((rows, model), bf16),
        grad_result=pltpu.VMEM((rows, model), bf16),
        grad_branch=pltpu.VMEM((rows, model), bf16),
        active=pltpu.VMEM((rows, hidden), bf16),
        grad_hidden=pltpu.VMEM((rows, hidden), bf16),
        qkv=pltpu.VMEM((rows, 3 * inner), bf16),
        grad_qkv=pltpu.VMEM((rows, 3 * inner), bf16),
        attended=pltpu.VMEM((rows, inner), bf16),
        grad_attended=pltpu.VMEM((rows, inner), bf16),
        middle=pltpu.VMEM((rows, model), f32),
        slope=pltpu.VMEM((rows, hidden), f32),
        table_sums=pltpu.VMEM((height, LANES), f32),
        own_table=pltpu.VMEM((height, LANES), bf16),
        all_table=pltpu.VMEM((peers, height, LANES), bf16),
        own_early=pltpu.VMEM((EARLY_LINES, LANES), f32),
        all_early=pltpu.VMEM((peers, EARLY_LINES, LANES), f32),
        own_late=pltpu.VMEM((peers, VECTORS, LANES), f32),
        all_late=pltpu.VMEM((peers, VECTORS, LANES), f32),
    )
    flat = jax.tree.leaves(arguments)
    near, apart = pl.BlockSpec(memory_space=pltpu.VMEM), pl.BlockSpec(memory_space=pl.ANY)
    specs = jax.tree.map(lambda _: near, arguments)
    specs.update(inputs=apart, out_grad=apart, large_index=apart)
    specs.update(slot_kind=pl.BlockSpec(memory_space=pltpu.SMEM))
    out_specs = jax.tree.map(lambda _: near, outs)
    out_specs.update(layer_out=apart)
    shapes, out_tree = jax.tree.flatten(outs)
    tree = jax.tree.structure((arguments, outs, scratch))
    results = pl.pallas_call(
        functools.partial(layer_body, (tree, heads, groups, slot_rows, peers)),
        out_shape=shapes,
        in_specs=jax.tree.leaves(specs),
        out_specs=jax.tree.leaves(out_specs),
        scratch_shapes=jax.tree.leaves(scratch),
        compiler_params=params(collective_id=0, has_side_effects=True),
        name="layer",
    )(*flat)
    return types.SimpleNamespace(**jax.tree.unflatten(out_tree, results))


def finish_body(tree, depth, *refs):
    found, out = (types.SimpleNamespace(**part) for part in jax.tree.unflatten(tree, refs))
    pairs = (
        (found.layer_out, out.layer_out),
        (found.input_grad, out.input_grad),
        (found.summed[1], out.fc1),
        (found.summed[2], out.fc2),
        (found.small_sums, out.small_table),
        (found.large_sums, out.large_table),
    )
    for src, dst in pairs:
        dst[...] = src[...]
    inner = out.query_bias.shape[0]
    for j in range(3):
        out.qkv[j] = found.summed[0][:, j * inner : (j + 1) * inner]
    out.out[...] = found.summed[0][:, 3 * inner :].T
    for i, vector in enumerate(out.vectors):
        vector[...] = found.late_sums[i, :depth]
    at = 1
    for line in (out.fc1_bias, out.query_bias, out.value_bias):
        size = line.shape[0]
        for first in range(0, size, LANES):
            count = min(LANES, size - first)
            line[pl.ds(first, count)] = found.early_sums[at, :count]
            at += 1


def finish(found, depth, inner, hidden):
    array = jax.ShapeDtypeStruct
    found = vars(found)
    outs = dict(
        layer_out=array(found["layer_out"].shape, bf16),
        input_grad=array(found["input_grad"].shape, bf16),
        fc1=array(found["summed"][1].shape, f32),
        fc2=array(found["summed"][2].shape, f32),
        small_table=array(found["small_sums"].shape, f32),
        large_table=array(found["large_sums"].shape, f32),
        qkv=array((3, depth, inner), f32),
        out=array((inner, depth), f32),
        vectors=[array((depth,), f32)] * VECTORS,
        fc1_bias=array((hidden,), f32),
        query_bias=array((inner,), f32),
        value_bias=array((inner,), f32),
    )
    shapes, out_tree = jax.tree.flatten(outs)
    results = pl.pallas_call(
        functools.partial(finish_body, jax.tree.structure((found, outs)), depth),
        out_shape=shapes,
        in_specs=in_vmem(len(jax.tree.leaves(found))),
        out_specs=in_vmem(len(shapes)),
        compiler_params=params(),
        name="finish",
    )(*jax.tree.leaves(found))
    return types.SimpleNamespace(**jax.tree.unflatten(out_tree, results))


def layer_norm(activations, norm_gain, norm_shift):
    center = activations - jnp.mean(activations, -1, keepdims=True)
    inverse = lax.rsqrt(jnp.mean(center * center, -1, keepdims=True) + EPS)
    normal = center * inverse
    return (normal * norm_gain + norm_shift, normal, inverse)


def norm_back(grad_normed, normal, inverse, norm_gain):
    scaled = grad_normed * norm_gain
    return inverse * (
        scaled
        - jnp.mean(scaled, -1, keepdims=True)
        - normal * jnp.mean(scaled * normal, -1, keepdims=True)
    )


def gelu_slope(hidden):
    cumulative = 0.5 * (1.0 + jax.scipy.special.erf(hidden * 0.7071067811865476))
    return cumulative + hidden * jnp.exp(-0.5 * hidden * hidden) * 0.3989422804014327


def pair_map(kind, small_index, large_index, rows, columns):
    def placed(index, at):
        side = index.shape[0]
        return jnp.pad(
            index, ((at, rows - at - side), (at, columns - at - side)), constant_values=-1
        )

    length = small_index.shape[0]
    small = placed(small_index, 0)
    for image in range(1, SLOT_ROWS // length):
        small = jnp.maximum(small, placed(small_index, image * length))
    return jnp.where(kind == 1, placed(large_index, 0), small)


def plain_device(
    images,
    out_grad,
    slot_kind,
    small_index,
    large_index,
    qkv_weight,
    out_weight,
    fc1_weight,
    fc2_weight,
    norm1_gain,
    norm1_shift,
    query_bias,
    value_bias,
    out_bias,
    gamma_attn,
    norm2_gain,
    norm2_shift,
    fc1_bias,
    fc2_bias,
    gamma_mlp,
    small_table,
    large_table,
):
    depth = qkv_weight.shape[0]
    width = query_bias.shape[0]
    hidden_width = fc1_bias.shape[0]
    heads = width // HEAD_DIM
    _, slot_rows, model_width = images.shape
    rows = up_to(slot_rows, 32)
    columns = up_to(rows, LANES)
    kind = slot_kind[0]

    block = jnp.concatenate(
        (
            qkv_weight.reshape(depth, 3 * width),
            fc1_weight,
            out_weight.T,
            fc2_weight.T,
        ),
        1,
    )
    whole = lax.all_gather(block, "dp", axis=0, tiled=True)
    cuts = (3 * width, 3 * width + hidden_width, 4 * width + hidden_width)
    qkv_matrix = whole[:, : cuts[0]]
    fc1_matrix = whole[:, cuts[0] : cuts[1]]
    out_turned = whole[:, cuts[1] : cuts[2]]
    fc2_turned = whole[:, cuts[2] :]
    small_vectors = jnp.stack(
        (norm1_gain, norm1_shift, out_bias, gamma_attn, norm2_gain, norm2_shift, fc2_bias, gamma_mlp)
    )
    vectors = lax.all_gather(small_vectors, "dp", axis=0)
    vectors = jnp.moveaxis(vectors, 0, 1).reshape(8, model_width).astype(f32)

    query_shift = query_bias.astype(f32)
    value_shift = value_bias.astype(f32)
    hidden_shift = fc1_bias.astype(f32)
    small_entries, large_entries = small_table.shape[0], large_table.shape[0]
    entries = up_to(max(small_entries, large_entries), LANES)
    table = jnp.where(
        kind == 1,
        jnp.pad(large_table, ((0, entries - large_entries), (0, 0))),
        jnp.pad(small_table, ((0, entries - small_entries), (0, 0))),
    )
    table = table.T.astype(f32)
    pair_index = pair_map(kind, small_index, large_index, rows, columns)
    bias = gather_bias(pair_index, table)

    positions = jnp.arange(rows)
    live_count = jnp.where(kind == 1, LARGE_LEN, slot_rows)
    live_rows = (positions < live_count).astype(f32).reshape(-1, 1)
    inputs = jnp.pad(images[0], ((0, rows - slot_rows), (0, 0))).astype(f32)
    normed_one, normal_one, inverse_one = layer_norm(inputs, vectors[0], vectors[1])
    normed_one = normed_one.astype(bf16)
    projected = dot(normed_one, qkv_matrix, 1, 0)
    queries = (projected[:, :width] + query_shift).astype(bf16)
    keys = projected[:, width : 2 * width].astype(bf16)
    values = (projected[:, 2 * width :] + value_shift).astype(bf16)
    pieces = attend_forward(queries, keys, values, bias)
    branch_part = dot(pieces, out_turned, 1, 1)
    branch = lax.psum(branch_part, "shard") + vectors[2]
    middle = inputs + vectors[3] * branch
    normed_two, normal_two, inverse_two = layer_norm(middle, vectors[4], vectors[5])
    normed_two = normed_two.astype(bf16)
    hidden = dot(normed_two, fc1_matrix, 1, 0) + hidden_shift
    active = jax.nn.gelu(hidden, approximate=False).astype(bf16)
    result_part = dot(active, fc2_turned, 1, 1)
    result = lax.psum(result_part.astype(bf16), "shard").astype(f32) + vectors[6]
    layer_out = ((middle + vectors[7] * result) * live_rows).astype(bf16)[:slot_rows][None]

    grad_out = jnp.pad(out_grad[0], ((0, rows - slot_rows), (0, 0))).astype(f32) * live_rows
    grad_gamma_mlp = jnp.sum(grad_out * result, 0)
    grad_result = (grad_out * vectors[7]).astype(bf16)
    grad_fc2_bias = jnp.sum(grad_result.astype(f32), 0)
    grad_fc2_turned = dot(grad_result, active, 0, 0)
    grad_active = dot(grad_result, fc2_turned, 1, 0)
    grad_hidden = (grad_active * gelu_slope(hidden)).astype(bf16)
    grad_fc1_bias = jnp.sum(grad_hidden.astype(f32), 0)
    grad_fc1 = dot(normed_two, grad_hidden, 0, 0)
    grad_normed_two = lax.psum(dot(grad_hidden, fc1_matrix, 1, 1), "shard")
    grad_norm2_gain = jnp.sum(grad_normed_two * normal_two, 0)
    grad_norm2_shift = jnp.sum(grad_normed_two, 0)
    grad_middle = grad_out + norm_back(grad_normed_two, normal_two, inverse_two, vectors[4])
    grad_gamma_attn = jnp.sum(grad_middle * branch, 0)
    grad_branch = (grad_middle * vectors[3]).astype(bf16)
    grad_out_bias = jnp.sum(grad_branch.astype(f32), 0)
    grad_out_turned = dot(grad_branch, pieces, 0, 0)
    grad_attended = dot(grad_branch, out_turned, 1, 0).astype(bf16)
    grad_queries, grad_keys, grad_values, grad_scores = attend_backward(
        queries, keys, values, bias, grad_attended
    )
    sums = table_sums(pair_index, grad_scores, entries)
    grad_projected = jnp.concatenate((grad_queries, grad_keys, grad_values), 1)
    grad_qkv = dot(normed_one, grad_projected, 0, 0)
    grad_query_bias = jnp.sum(grad_queries.astype(f32), 0)
    grad_value_bias = jnp.sum(grad_values.astype(f32), 0)
    grad_normed_one = lax.psum(dot(grad_projected, qkv_matrix, 1, 1), "shard")
    grad_norm1_gain = jnp.sum(grad_normed_one * normal_one, 0)
    grad_norm1_shift = jnp.sum(grad_normed_one, 0)
    input_grad = grad_middle + norm_back(grad_normed_one, normal_one, inverse_one, vectors[0])
    input_grad = input_grad.astype(bf16)[:slot_rows][None]

    small_sums = jnp.where(kind == 1, 0.0, sums[:, :small_entries])
    large_sums = jnp.where(kind == 1, sums[:, :large_entries], 0.0)
    local_sums = lax.psum(
        (small_sums, large_sums, grad_query_bias, grad_value_bias, grad_fc1_bias), "dp"
    )
    peers = lax.axis_size("dp")

    def sent_and_summed(value):
        parts = value.astype(bf16).reshape(peers, value.shape[0] // peers, -1)
        arrived = lax.all_to_all(parts, "dp", split_axis=0, concat_axis=0, tiled=True)
        return arrived.astype(f32).sum(axis=0)

    grad_block = sent_and_summed(
        jnp.concatenate((grad_qkv, grad_fc1, grad_out_turned, grad_fc2_turned), 1)
    )
    vector_grads = sent_and_summed(
        jnp.stack(
            (
                grad_norm1_gain,
                grad_norm1_shift,
                grad_out_bias,
                grad_gamma_attn,
                grad_norm2_gain,
                grad_norm2_shift,
                grad_fc2_bias,
                grad_gamma_mlp,
            ),
            1,
        )
    )
    return (
        layer_out,
        input_grad,
        grad_block[:, : cuts[0]].reshape(depth, 3, width),
        grad_block[:, cuts[1] : cuts[2]].T,
        grad_block[:, cuts[0] : cuts[1]],
        grad_block[:, cuts[2] :].T,
        vector_grads[:, 0],
        vector_grads[:, 1],
        local_sums[2],
        local_sums[3],
        vector_grads[:, 2],
        vector_grads[:, 3],
        vector_grads[:, 4],
        vector_grads[:, 5],
        local_sums[4],
        vector_grads[:, 6],
        vector_grads[:, 7],
        local_sums[0].T,
        local_sums[1].T,
    )


def on_device(*arguments):
    depth = arguments[5].shape[0]
    if depth % 16 or lax.axis_size("shard") != 4:
        return plain_device(*arguments)
    return whole_device(*arguments)


def whole_device(
    images,
    out_grad,
    slot_kind,
    small_index,
    large_index,
    qkv_weight,
    out_weight,
    fc1_weight,
    fc2_weight,
    norm1_gain,
    norm1_shift,
    query_bias,
    value_bias,
    out_bias,
    gamma_attn,
    norm2_gain,
    norm2_shift,
    fc1_bias,
    fc2_bias,
    gamma_mlp,
    small_table,
    large_table,
):
    depth = qkv_weight.shape[0]
    found = layer(
        dict(
            inputs=images[0],
            out_grad=out_grad[0],
            slot_kind=slot_kind,
            small_index=small_index,
            large_index=large_index,
            small_table=small_table.T,
            large_table=large_table.T,
            qkv_weight=qkv_weight.transpose(1, 0, 2),
            out_weight=out_weight,
            fc1_weight=fc1_weight,
            fc2_weight=fc2_weight.T,
            small_vectors=[
                norm1_gain,
                norm1_shift,
                out_bias,
                gamma_attn,
                norm2_gain,
                norm2_shift,
                fc2_bias,
                gamma_mlp,
            ],
            query_bias=query_bias,
            value_bias=value_bias,
            fc1_bias=fc1_bias,
        ),
        lax.axis_size("dp"),
        images.shape[1],
    )
    out = finish(found, depth, query_bias.shape[0], fc1_bias.shape[0])
    return (
        out.layer_out[None],
        out.input_grad[None],
        out.qkv.transpose(1, 0, 2),
        out.out,
        out.fc1,
        out.fc2.T,
        out.vectors[6],
        out.vectors[7],
        out.query_bias,
        out.value_bias,
        out.vectors[0],
        out.vectors[1],
        out.vectors[2],
        out.vectors[3],
        out.fc1_bias,
        out.vectors[4],
        out.vectors[5],
        out.small_table.T,
        out.large_table.T,
    )


def solution(mesh):
    return jax.shard_map(
        on_device,
        mesh=mesh,
        in_specs=(
            P("dp", None, None),
            P("dp", None, None),
            P("dp"),
            P(),
            P(),
            P("dp", None, "shard"),
            P("shard", "dp"),
            P("dp", "shard"),
            P("shard", "dp"),
            P("dp"),
            P("dp"),
            P("shard"),
            P("shard"),
            P("dp"),
            P("dp"),
            P("dp"),
            P("dp"),
            P("shard"),
            P("dp"),
            P("dp"),
            P(None, "shard"),
            P(None, "shard"),
        ),
        out_specs=(
            P("dp", None, None),
            P("dp", None, None),
            P("dp", None, "shard"),
            P("shard", "dp"),
            P("dp", "shard"),
            P("shard", "dp"),
            P("dp"),
            P("dp"),
            P("shard"),
            P("shard"),
            P("dp"),
            P("dp"),
            P("dp"),
            P("dp"),
            P("shard"),
            P("dp"),
            P("dp"),
            P(None, "shard"),
            P(None, "shard"),
        ),
        check_vma=False,
    )
```

profile of v0, /device:TPU:0, one launch (start us, length us, event | category | flops | bytes accessed | tf_op | source)
XLA Modules:
  0.0 156.0 jit_solution(6442310207000748900)
XLA Ops:
  1.3 151.0 %layer.1 = (f32[16,128]{1,0:T(8,128)}, bf16[591,768]{1,0:T(8,128)(2,1)}, f32[3,2212]{1,0:T(4,128)}, f32[8,128]{1,0:T(8,128)}, bf16[591,768]{1,0:T(8,128)(2,1)}, ...) custom-call(bf16[768]{0:T(1024)(128)(2,1)} %refs_0_.1, bf16[96,768]{1,0:T(8,128)(2,1)} %refs_1_.1, ...), custom_call_target="tpu_custom_call" | custom-call | tf_op jit(solution)/shard_map/layer/pallas_call | solution.py:1120
  152.3 3.5 %finish.1 = (f32[96,768]{1,0:T(8,128)}, f32[768]{0:T(1024)}, f32[96,768]{1,0:T(8,128)}, bf16[591,768]{1,0:T(8,128)(2,1)}, f32[3,2212]{1,0:T(4,128)}, /*index=5*/...) custom-call(f32[16,128]{1,0:T(8,128)} %get-tuple-element.47.refs_0_,, ...), custom_call_target="tpu_custom_call" | custom-call | tf_op jit(solution)/shard_map/finish/pallas_call | solution.py:1177
where the time goes:
time: 156 us
  Pallas kernels  154 us (99%)
    pallas_call x1, Pallas kernels, layer(): pl.pallas_call(functools.partial(layer_body, (tree, heads, groups, slot_r...  151 us
    pallas_call x1, Pallas kernels, finish(): pl.pallas_call(functools.partial(finish_body, jax.tree.structure((found,...  3.47 us

commit v1 on v0

--- a/solution.py
+++ b/solution.py
@@ -16,7 +16,7 @@
 NEG = -1e30
 LANES = 128
 SPLIT = 80
-VMEM_LIMIT = 56 << 20
+VMEM_LIMIT = 60 << 20
 
 MESH = pl.DeviceIdType.MESH
 
@@ -531,11 +531,12 @@
 CHUNKS = 5
 VECTORS = 8
 EARLY_LINES = 16
-LAG = 0
 BIAS_PLACES = [5, 11, 17, 11, 19, 25, 32, 20, 28, 36, 99]
 TABLE_PLACES = [1, 3, 10, 15, 20, 24, 30, 36, 99]
-CLOSE_PLACE = 17
-NORM_PLACE = 22
+FIRST_CLOSE = 2
+RESULT_PLACE = 7
+CLOSE_PLACE = 22
+NORM_PLACE = 27
 
 
 def with_events(blocks, events, work):
@@ -811,15 +812,7 @@
             floods[2].arrive()
         put(r.part[1], c, dot(active, r.whole[2][...], 1, 1))
         sums[1].first(c).start()
-
-    def turn(c):
-        sums[1].third(c).wait_recv()
-        result = both(r.total[1], c) + vector(6)
-        live = live_rows(c)
-        keep(r.out_here, c, (live * (both(r.middle, c) + vector(7) * result)).astype(bf16))
-        grad = padded(r.grad_here, c) * live
-        add(6, grad * result)
-        grad_result = (grad * vector(7)).astype(bf16)
+        grad_result = (padded(r.grad_here, c) * live_rows(c) * vector(7)).astype(bf16)
         put(r.grad_result, c, grad_result)
         add(5, grad_result.astype(f32))
         grad_hidden = (dot(grad_result, r.whole[2][...], 1, 0) * both(r.slope, c)).astype(bf16)
@@ -827,6 +820,16 @@
         add(0, grad_hidden.astype(f32))
         put(r.part[2], c, dot(grad_hidden, r.whole[1][...], 1, 1))
         sums[2].first(c).start()
+
+    def results():
+        for c in range(count):
+            sums[1].third(c).wait_recv()
+            result = both(r.total[1], c) + vector(6)
+            live = live_rows(c)
+            keep(r.out_here, c, (live * (both(r.middle, c) + vector(7) * result)).astype(bf16))
+            add(6, padded(r.grad_here, c) * live * result)
+        to_owners(5, r.running[6])
+        store.start()
 
     def back_norm(grad, normal, inverse, gain):
         scaled = grad * gain
@@ -842,7 +845,7 @@
         add(4, grad)
         grad_middle = padded(r.grad_here, c) * live_rows(c)
         grad_middle = grad_middle + back_norm(grad, normal, inverse, vector(4))
-        put(r.middle, c, grad_middle)
+        put(r.grad_middle, c, grad_middle)
         add(2, grad_middle * (both(r.total[0], c) + vector(2)))
         grad_branch = (grad_middle * vector(3)).astype(bf16)
         put(r.grad_branch, c, grad_branch)
@@ -855,8 +858,8 @@
     def cross(work):
         return lambda c: work.cross_one(c)
 
-    stages = [project, cross(sums[0]), close(sums[0]), forward, cross(sums[1]), close(sums[1])]
-    stages += [turn, cross(sums[2]), close(sums[2]), backward]
+    stages = [project, cross(sums[0]), close(sums[0]), forward]
+    stages += [cross(sums[2]), close(sums[2]), backward]
 
     def weight_grad(j, left, right, at=0):
         value = dot(left[...], right[...], 0, 0).astype(bf16)
@@ -866,20 +869,19 @@
         for s in range(length - 1, -1, -1):
             scatters[j].start(s)
 
-    slots = [0, 1, 2] + [k + LAG for k in range(3, 6)] + [k + 2 * LAG for k in range(6, 10)]
-    for t in range(count + slots[-1]):
+    for t in range(count + len(stages) - 1):
         for k in range(len(stages) - 1, -1, -1):
-            if 0 <= t - slots[k] < count:
-                stages[k](t - slots[k])
-        if t == count + slots[6]:
+            if 0 <= t - k < count:
+                stages[k](t - k)
+        if t == count + 2:
             weight_grad(2, r.grad_result, r.active)
             send_grads(2)
-        if t == count + slots[7]:
+        if t == count + 3:
+            sums[1].cross()
             weight_grad(1, r.normed[1], r.grad_hidden)
             send_grads(1)
 
     store = pltpu.make_async_copy(r.out_here, r.layer_out, r.load_sem.at[0])
-    store.start()
     weight_grad(0, r.grad_branch, r.attended, 3 * inner)
     steps = list(range(length - 1, -1, -1))
     for h in range(heads):
@@ -931,7 +933,7 @@
             r.own_late[d, i : i + 1, :depth] = line[:, d * depth : (d + 1) * depth]
 
     r.own_late[...] = jnp.zeros_like(r.own_late)
-    for i in range(1, 7):
+    for i in range(1, 6):
         to_owners(i - 1, r.running[i])
     r.table_sums[...] = jnp.zeros_like(r.table_sums)
 
@@ -939,7 +941,7 @@
         grad = r.total[0][here]
         normal = (r.kept[here].astype(f32) - r.mean[0][here]) * r.inverse[0][here]
         back = back_norm(grad, normal, r.inverse[0][here], vector(0))
-        value = (r.middle[here] + back).astype(bf16)
+        value = (r.grad_middle[here] + back).astype(bf16)
         if out_rows is None:
             r.input_grad[here] = value
         else:
@@ -969,7 +971,9 @@
     order += [(j, s) for j in (1, 0) for s in steps]
     places = TABLE_PLACES if length == 4 else [4 * k for k in range(len(order))]
     events = [(at, scatter_event(*item)) for at, item in zip(places, order)]
-    events += [(0, last.cross), (CLOSE_PLACE, last.close), (NORM_PLACE, norm_rows)]
+    events += [(0, last.cross), (FIRST_CLOSE, sums[1].close), (RESULT_PLACE, results)]
+    events += [(CLOSE_PLACE, last.close), (NORM_PLACE, norm_rows)]
+    events.sort(key=lambda item: item[0])
     with_events(
         blocks,
         [(at, event) for at, event in events if at < blocks],
@@ -1099,6 +1103,7 @@
         attended=pltpu.VMEM((rows, inner), bf16),
         grad_attended=pltpu.VMEM((rows, inner), bf16),
         middle=pltpu.VMEM((rows, model), f32),
+        grad_middle=pltpu.VMEM((rows, model), f32),
         slope=pltpu.VMEM((rows, hidden), f32),
         table_sums=pltpu.VMEM((height, LANES), f32),
         own_table=pltpu.VMEM((height, LANES), bf16),

time: 156 us -> 148 us (0.949)
  Pallas kernels: 154 us -> 146 us
    pallas_call x1, Pallas kernels: 151 us -> 143 us  [layer(): pl.pallas_call(functools.partial(layer_body, (tree, heads, groups, slot_r...]
where the time goes in v1:
time: 148 us
  Pallas kernels  146 us (99%)
  between operations  1.5 us (1%)
    pallas_call x1, Pallas kernels, layer(): pl.pallas_call(functools.partial(layer_body, (tree, heads, groups, slot_r...  143 us
    pallas_call x1, Pallas kernels, finish(): pl.pallas_call(functools.partial(finish_body, jax.tree.structure((found,...  3.47 us

profile of v1, /device:TPU:0, one launch (start us, length us, event | category | flops | bytes accessed | tf_op | source)
XLA Modules:
  0.0 147.6 jit_solution(9340881586441312909)
XLA Ops:
  1.3 142.6 %layer.1 = (f32[16,128]{1,0:T(8,128)}, bf16[591,768]{1,0:T(8,128)(2,1)}, f32[3,2212]{1,0:T(4,128)}, f32[8,128]{1,0:T(8,128)}, bf16[591,768]{1,0:T(8,128)(2,1)}, ...) custom-call(bf16[768]{0:T(1024)(128)(2,1)} %refs_0_.1, bf16[96,768]{1,0:T(8,128)(2,1)} %refs_1_.1, ...), custom_call_target="tpu_custom_call" | custom-call | tf_op jit(solution)/shard_map/layer/pallas_call | solution.py:1125
  143.9 3.5 %finish.1 = (f32[96,768]{1,0:T(8,128)}, f32[768]{0:T(1024)}, f32[96,768]{1,0:T(8,128)}, bf16[591,768]{1,0:T(8,128)(2,1)}, f32[3,2212]{1,0:T(4,128)}, /*index=5*/...) custom-call(f32[16,128]{1,0:T(8,128)} %get-tuple-element.47.refs_0_,, ...), custom_call_target="tpu_custom_call" | custom-call | tf_op jit(solution)/shard_map/finish/pallas_call | solution.py:1182

commit v2 on v1

--- a/solution.py
+++ b/solution.py
@@ -528,11 +528,11 @@
 
 
 ROW_STEP = 16
-CHUNKS = 5
+CHUNKS = 4
 VECTORS = 8
 EARLY_LINES = 16
-BIAS_PLACES = [5, 11, 17, 11, 19, 25, 32, 20, 28, 36, 99]
-TABLE_PLACES = [1, 3, 10, 15, 20, 24, 30, 36, 99]
+BIAS_PLACES = [4, 14, 24, 18, 32, 99, 7, 25, 36, 99]
+TABLE_PLACES = [-1, 6, 31, 2, 10, 21, 44, 16, 26, 29, 39]
 FIRST_CLOSE = 2
 RESULT_PLACE = 7
 CLOSE_PLACE = 22
@@ -636,6 +636,7 @@
     pl.semaphore_wait(barrier, met + peers - 1)
     lines.step(0)
     floods[0].step(0)
+    floods[1].step(0)
     copies = [
         pltpu.make_async_copy(flood.own, flood.at(grid.me), r.local_sem.at[j])
         for j, flood in enumerate(floods + [lines])
@@ -693,7 +694,8 @@
     def flood_event(j, s):
         return lambda: floods[j].step(s)
 
-    order = [(0, s) for s in range(1, length)] + [(j, s) for j in (1, 2) for s in range(length)]
+    order = [(j, s) for j in range(2) for s in range(1, length)]
+    order += [(2, s) for s in range(length)]
     places = BIAS_PLACES if length == 4 else [k * 3 for k in range(len(order))]
     events = [(at, flood_event(*item)) for at, item in zip(places, order)]
     events += [(3 * s, functools.partial(lines.step, s)) for s in range(1, length)]
@@ -752,7 +754,7 @@
         return weights * (1.0 / jnp.sum(weights, -1, keepdims=True))
 
     for h in range(heads):
-        for event in late_floods[h * len(late_floods) // heads : (h + 1) * len(late_floods) // heads]:
+        for event in late_floods if h == heads - 1 else ():
             event()
         part = slice(h * HEAD_DIM, (h + 1) * HEAD_DIM)
         values = slice(2 * inner + h * HEAD_DIM, 2 * inner + (h + 1) * HEAD_DIM)
@@ -897,8 +899,19 @@
         r.bias[h, :, :rows] = grad
         r.grad_qkv[:, part] = (dot(grad, r.qkv[:, keys], 1, 0) * factor).astype(bf16)
         r.grad_qkv[:, keys] = (dot(grad, r.qkv[:, part], 0, 0) * factor).astype(bf16)
-        if h + 1 < length:
-            scatters[2].step(steps[h])
+        if h == 0:
+            scatters[2].step(steps[0])
+
+    def scatter_event(j, s):
+        return lambda: scatters[j].step(s)
+
+    order = [(2, s) for s in steps[1:]] + [(j, s) for j in (1, 0) for s in steps]
+    places = TABLE_PLACES if length == 4 else [4 * k for k in range(len(order))]
+    events = [(at, scatter_event(*item)) for at, item in zip(places, order)]
+    for at, event in events:
+        if at < 0:
+            event()
+    events = [(at, event) for at, event in events if at >= 0]
 
     sums[0].drain()
     last = sums[0]
@@ -964,13 +977,6 @@
         to_owners(6, gain)
         to_owners(7, shift)
 
-    def scatter_event(j, s):
-        return lambda: scatters[j].step(s)
-
-    order = [(2, s) for s in steps[min(heads, length - 1) :]]
-    order += [(j, s) for j in (1, 0) for s in steps]
-    places = TABLE_PLACES if length == 4 else [4 * k for k in range(len(order))]
-    events = [(at, scatter_event(*item)) for at, item in zip(places, order)]
     events += [(0, last.cross), (FIRST_CLOSE, sums[1].close), (RESULT_PLACE, results)]
     events += [(CLOSE_PLACE, last.close), (NORM_PLACE, norm_rows)]
     events.sort(key=lambda item: item[0])

time: 148 us -> 139 us (0.939)
  Pallas kernels: 146 us -> 137 us
    pallas_call x1, Pallas kernels: 143 us -> 134 us  [layer(): pl.pallas_call(functools.partial(layer_body, (tree, heads, groups, slot_r...]
where the time goes in v2:
time: 139 us
  Pallas kernels  137 us (99%)
  between operations  1.5 us (1%)
    pallas_call x1, Pallas kernels, layer(): pl.pallas_call(functools.partial(layer_body, (tree, heads, groups, slot_r...  134 us
    pallas_call x1, Pallas kernels, finish(): pl.pallas_call(functools.partial(finish_body, jax.tree.structure((found,...  3.47 us

profile of v2, /device:TPU:0, one launch (start us, length us, event | category | flops | bytes accessed | tf_op | source)
XLA Modules:
  0.0 138.7 jit_solution(5704829612770665039)
XLA Ops:
  1.3 133.8 %layer.1 = (f32[16,128]{1,0:T(8,128)}, bf16[591,768]{1,0:T(8,128)(2,1)}, f32[3,2212]{1,0:T(4,128)}, f32[8,128]{1,0:T(8,128)}, bf16[591,768]{1,0:T(8,128)(2,1)}, ...) custom-call(bf16[768]{0:T(1024)(128)(2,1)} %refs_0_.1, bf16[96,768]{1,0:T(8,128)(2,1)} %refs_1_.1, ...), custom_call_target="tpu_custom_call" | custom-call | tf_op jit(solution)/shard_map/layer/pallas_call | solution.py:1131
  135.1 3.5 %finish.1 = (f32[96,768]{1,0:T(8,128)}, f32[768]{0:T(1024)}, f32[96,768]{1,0:T(8,128)}, bf16[591,768]{1,0:T(8,128)(2,1)}, f32[3,2212]{1,0:T(4,128)}, /*index=5*/...) custom-call(f32[16,128]{1,0:T(8,128)} %get-tuple-element.47.refs_0_,, ...), custom_call_target="tpu_custom_call" | custom-call | tf_op jit(solution)/shard_map/finish/pallas_call | solution.py:1188

commit v3 on v2

--- a/solution.py
+++ b/solution.py
@@ -758,7 +758,8 @@
             event()
         part = slice(h * HEAD_DIM, (h + 1) * HEAD_DIM)
         values = slice(2 * inner + h * HEAD_DIM, 2 * inner + (h + 1) * HEAD_DIM)
-        r.attended[:, part] = dot(weights_of(h).astype(bf16), r.qkv[:, values], 1, 0).astype(bf16)
+        r.bias[h, :, :rows] = weights_of(h).astype(bf16)
+        r.attended[:, part] = dot(r.bias[h, :, :rows], r.qkv[:, values], 1, 0).astype(bf16)
 
     def out_turned():
         return r.whole[0][:, 3 * inner :]
@@ -890,9 +891,9 @@
         part = slice(h * HEAD_DIM, (h + 1) * HEAD_DIM)
         keys = slice(inner + h * HEAD_DIM, inner + (h + 1) * HEAD_DIM)
         values = slice(2 * inner + h * HEAD_DIM, 2 * inner + (h + 1) * HEAD_DIM)
-        weights = weights_of(h)
         grad_part = r.grad_attended[:, part]
-        r.grad_qkv[:, values] = dot(weights.astype(bf16), grad_part, 0, 0).astype(bf16)
+        r.grad_qkv[:, values] = dot(r.bias[h, :, :rows], grad_part, 0, 0).astype(bf16)
+        weights = r.bias[h, :, :rows].astype(f32)
         grad = dot(grad_part, r.qkv[:, values], 1, 1)
         mean = jnp.sum(weights * grad, -1, keepdims=True)
         grad = (weights * (grad - mean)).astype(bf16)

time: 139 us -> 138 us (level)
  no operation moved by 1% of the time
where the time goes in v3:
time: 138 us
  Pallas kernels  136 us (99%)
  between operations  1.5 us (1%)
    pallas_call x1, Pallas kernels, layer(): pl.pallas_call(functools.partial(layer_body, (tree, heads, groups, slot_r...  133 us
    pallas_call x1, Pallas kernels, finish(): pl.pallas_call(functools.partial(finish_body, jax.tree.structure((found,...  3.47 us

profile of v3, /device:TPU:0, one launch (start us, length us, event | category | flops | bytes accessed | tf_op | source)
XLA Modules:
  0.0 137.7 jit_solution(15474240738649590747)
XLA Ops:
  1.3 132.8 %layer.1 = (f32[16,128]{1,0:T(8,128)}, bf16[591,768]{1,0:T(8,128)(2,1)}, f32[3,2212]{1,0:T(4,128)}, f32[8,128]{1,0:T(8,128)}, bf16[591,768]{1,0:T(8,128)(2,1)}, ...) custom-call(bf16[768]{0:T(1024)(128)(2,1)} %refs_0_.1, bf16[96,768]{1,0:T(8,128)(2,1)} %refs_1_.1, ...), custom_call_target="tpu_custom_call" | custom-call | tf_op jit(solution)/shard_map/layer/pallas_call | solution.py:1132
  134.1 3.5 %finish.1 = (f32[96,768]{1,0:T(8,128)}, f32[768]{0:T(1024)}, f32[96,768]{1,0:T(8,128)}, bf16[591,768]{1,0:T(8,128)(2,1)}, f32[3,2212]{1,0:T(4,128)}, /*index=5*/...) custom-call(f32[16,128]{1,0:T(8,128)} %get-tuple-element.47.refs_0_,, ...), custom_call_target="tpu_custom_call" | custom-call | tf_op jit(solution)/shard_map/finish/pallas_call | solution.py:1189

commit v4 on v3

--- a/solution.py
+++ b/solution.py
@@ -754,12 +754,13 @@
         return weights * (1.0 / jnp.sum(weights, -1, keepdims=True))
 
     for h in range(heads):
-        for event in late_floods if h == heads - 1 else ():
-            event()
         part = slice(h * HEAD_DIM, (h + 1) * HEAD_DIM)
         values = slice(2 * inner + h * HEAD_DIM, 2 * inner + (h + 1) * HEAD_DIM)
         r.bias[h, :, :rows] = weights_of(h).astype(bf16)
         r.attended[:, part] = dot(r.bias[h, :, :rows], r.qkv[:, values], 1, 0).astype(bf16)
+
+    for event in late_floods:
+        event()
 
     def out_turned():
         return r.whole[0][:, 3 * inner :]
@@ -977,6 +978,7 @@
             gain, shift = gain + more[0], shift + more[1]
         to_owners(6, gain)
         to_owners(7, shift)
+        spreads[1].start(lambda peer: r.own_late.at[peer])
 
     events += [(0, last.cross), (FIRST_CLOSE, sums[1].close), (RESULT_PLACE, results)]
     events += [(CLOSE_PLACE, last.close), (NORM_PLACE, norm_rows)]
@@ -995,7 +997,6 @@
     )
     r.own_table[...] = r.table_sums[...].astype(bf16)
     spreads[2].start(lambda peer: r.own_table)
-    spreads[1].start(lambda peer: r.own_late.at[peer])
     for at, event in events:
         if at >= blocks:
             event()

time: 138 us -> 135 us (0.978)
  Pallas kernels: 136 us -> 134 us
    pallas_call x1, Pallas kernels: 133 us -> 130 us  [layer(): pl.pallas_call(functools.partial(layer_body, (tree, heads, groups, slot_r...]
where the time goes in v4:
time: 135 us
  Pallas kernels  134 us (99%)
  between operations  1.5 us (1%)
    pallas_call x1, Pallas kernels, layer(): pl.pallas_call(functools.partial(layer_body, (tree, heads, groups, slot_r...  130 us
    pallas_call x1, Pallas kernels, finish(): pl.pallas_call(functools.partial(finish_body, jax.tree.structure((found,...  3.47 us

profile of v4, /device:TPU:0, one launch (start us, length us, event | category | flops | bytes accessed | tf_op | source)
XLA Modules:
  0.0 135.3 jit_solution(18067632147373107709)
XLA Ops:
  1.3 130.3 %layer.1 = (f32[16,128]{1,0:T(8,128)}, bf16[591,768]{1,0:T(8,128)(2,1)}, f32[3,2212]{1,0:T(4,128)}, f32[8,128]{1,0:T(8,128)}, bf16[591,768]{1,0:T(8,128)(2,1)}, ...) custom-call(bf16[768]{0:T(1024)(128)(2,1)} %refs_0_.1, bf16[96,768]{1,0:T(8,128)(2,1)} %refs_1_.1, ...), custom_call_target="tpu_custom_call" | custom-call | tf_op jit(solution)/shard_map/layer/pallas_call | solution.py:1133
  131.6 3.5 %finish.1 = (f32[96,768]{1,0:T(8,128)}, f32[768]{0:T(1024)}, f32[96,768]{1,0:T(8,128)}, bf16[591,768]{1,0:T(8,128)(2,1)}, f32[3,2212]{1,0:T(4,128)}, /*index=5*/...) custom-call(f32[16,128]{1,0:T(8,128)} %get-tuple-element.47.refs_0_,, ...), custom_call_target="tpu_custom_call" | custom-call | tf_op jit(solution)/shard_map/finish/pallas_call | solution.py:1190
